TPU v7x, 256 devices: a whole 4x4x8 slice. The times are simulated.
256 devices in a mesh: rep: 2 (over z_hi), dp: 32 (over z_lo, x, core), mp: 4 (over y).
Axes of the slice: x: 4, y: 4, z: 8 (z_hi: 2, z_lo: 4; z = z_hi * 4 + z_lo), core: 2. Of those that a mesh axis runs over, the one named last changes fastest.
Arguments:
- tokens: bfloat16 [24576, 2048], P(('rep', 'dp', 'mp')), may hold values from -6 to 6
- request_ids: int32 [64, 384], P(('rep', 'dp')), may hold values from 0 to 7, never falling along the last dimension, each value on 1 to 192 neighbouring positions
- cache_entries: bfloat16 [32768, 4096], P(('rep', 'dp', 'mp')), may hold values from -250 to 250, as said below
- cached_lengths: int32 [64, 8], replicated, may hold values from 1 to 256, 512 in all within a row
- traded: int32 [32], P('dp'), may hold values from 0 to 1, as said below
- query_weight: bfloat16 [2048, 2048], P(None, 'mp'), may hold values from -0.125 to 0.125
- key_weight: bfloat16 [2048, 2048], P(None, 'mp'), may hold values from -0.125 to 0.125
- value_weight: bfloat16 [2048, 2048], P(None, 'mp'), may hold values from -0.125 to 0.125
- output_weight: bfloat16 [2048, 2048], P('mp'), may hold values from -0.125 to 0.125
- gate_weight: bfloat16 [2048, 8192], P('dp', 'mp'), may hold values from -0.125 to 0.125
- up_weight: bfloat16 [2048, 8192], P('dp', 'mp'), may hold values from -0.125 to 0.125
- down_weight: bfloat16 [2048, 8192], P('dp', 'mp'), may hold values from -0.0625 to 0.0625
Outputs:
- layer_output: bfloat16 [24576, 2048], P(('rep', 'dp', 'mp'))
Inputs may be any that keep to these rules, and one draw needn't show every extreme that they name: `request_ids`: each group's row never falls; every request 0 to 7 has 1 to 192 new tokens in each group, some request exactly 192. `cached_lengths`: each row sums to 512; its largest entry is 256. `traded`: exactly 16 entries are 1. `cache_entries`: keys are stored already rotated to their positions; rows of cache group g are g * 512 to (g + 1) * 512 - 1, the requests' prefixes in request order.
All inputs are finite; a program needn't handle non-finite values.
Results may differ from a plain program's by a relative error of at most 0.013.
The roundings to bfloat16 on the way count: a program that leaves them out, or rounds other values in their place, can miss the bound.
Values may be sent and summed in bfloat16 or wider, within the bound.
A program may use at most 128 MiB of HBM per device.

v0:
```python
import math
import jax
import jax.numpy as jnp
from jax import lax
from jax.sharding import PartitionSpec as P

D = 2048
HEADS = 16
HEAD_DIM = 128
TOK_GROUP = 384
CACHE = 512
EPSILON = 1e-05
ROPE_BASE = 10000.0


def swapped(value, axis, apart):
    mask = 2**apart
    pairs = [(source, source ^ mask) for source in range(lax.axis_size(axis))]
    return lax.ppermute(value, axis, pairs)


def layer_norm(rows):
    center = rows - jnp.mean(rows, axis=-1, keepdims=True)
    spread = jnp.mean(center * center, axis=-1, keepdims=True)
    return center * lax.rsqrt(spread + EPSILON)


def request_layout(request_row, length_row, cache_size):
    number = length_row.shape[0]
    labels = jnp.arange(number, dtype=jnp.int32)
    onehot = (request_row[:, None] == labels[None, :]).astype(jnp.int32)
    counts = jnp.sum(onehot, axis=0)
    starts = jnp.cumsum(counts) - counts
    token_place = jnp.arange(request_row.shape[0], dtype=jnp.int32)
    positions = jnp.sum(onehot * (length_row - starts)[None, :], axis=1) + token_place
    bounds = jnp.cumsum(length_row)
    cache_place = jnp.arange(cache_size, dtype=jnp.int32)
    owner = jnp.sum((cache_place[:, None] >= bounds[None, :]).astype(jnp.int32), axis=1)
    return (positions, owner)


def rotate(vectors, positions):
    half = vectors.shape[-1] // 2
    freq = ROPE_BASE ** (-jnp.arange(half, dtype=jnp.float32) / half)
    angle = positions.astype(jnp.float32)[:, None] * freq[None, :]
    cosine = jnp.cos(angle)[:, None, :]
    sine = jnp.sin(angle)[:, None, :]
    first = vectors[..., :half]
    second = vectors[..., half:]
    return jnp.concatenate(
        [first * cosine - second * sine, second * cosine + first * sine], axis=-1
    )


def attend(query, keys_new, values_new, keys_cache, values_cache, request_row, owner):
    scale = 1.0 / math.sqrt(query.shape[-1])
    keys = jnp.concatenate([keys_cache, keys_new], axis=0)
    values = jnp.concatenate([values_cache, values_new], axis=0)
    scores = jnp.einsum("thd,khd->htk", query, keys, preferred_element_type=jnp.float32) * scale
    count = request_row.shape[0]
    place = jnp.arange(count, dtype=jnp.int32)
    same_cache = owner[None, :] == request_row[:, None]
    same_new = (request_row[None, :] == request_row[:, None]) & (place[None, :] <= place[:, None])
    allowed = jnp.concatenate([same_cache, same_new], axis=1)
    scores = jnp.where(allowed[None], scores, -1e30)
    top = jnp.max(scores, axis=-1, keepdims=True)
    raised = jnp.exp(scores - top)
    total = jnp.sum(raised, axis=-1, keepdims=True)
    weights = (raised / total).astype(jnp.bfloat16)
    mixed = jnp.einsum("htk,khd->thd", weights, values, preferred_element_type=jnp.float32)
    return mixed.astype(jnp.bfloat16)


def local(
    tokens,
    request_ids,
    cache_entries,
    cached_lengths,
    traded,
    query_weight,
    key_weight,
    value_weight,
    output_weight,
    gate_weight,
    up_weight,
    down_weight,
):
    tensor_size = lax.axis_size("mp")
    local_heads = HEADS // tensor_size
    replica = lax.axis_index("rep")
    within = lax.axis_index("dp")
    pairs = lax.axis_size("dp")
    group = replica * pairs + within
    moved_here = traded[0] == 1
    source = jnp.where(moved_here, (1 - replica) * pairs + within, group)
    length_row = lax.dynamic_slice_in_dim(cached_lengths, source, 1, 0)[0]
    request_row = request_ids[0]
    partner = swapped(cache_entries, "rep", 0)
    stored = jnp.where(moved_here, partner, cache_entries)
    by_heads = lax.all_to_all(
        stored.reshape(stored.shape[0], 2, D), "mp", split_axis=2, concat_axis=0, tiled=True
    )
    keys_cache = by_heads[:, 0].reshape(CACHE, local_heads, HEAD_DIM)
    values_cache = by_heads[:, 1].reshape(CACHE, local_heads, HEAD_DIM)
    rows_full = lax.all_gather(tokens, "mp", axis=0, tiled=True)
    positions, owner = request_layout(request_row, length_row, CACHE)
    normed = layer_norm(rows_full.astype(jnp.float32)).astype(jnp.bfloat16)
    query = jnp.dot(normed, query_weight, preferred_element_type=jnp.float32).reshape(
        TOK_GROUP, local_heads, HEAD_DIM
    )
    query = rotate(query, positions).astype(jnp.bfloat16)
    keys_new = jnp.dot(normed, key_weight, preferred_element_type=jnp.float32).reshape(
        TOK_GROUP, local_heads, HEAD_DIM
    )
    keys_new = rotate(keys_new, positions).astype(jnp.bfloat16)
    values_new = (
        jnp.dot(normed, value_weight, preferred_element_type=jnp.float32)
        .astype(jnp.bfloat16)
        .reshape(TOK_GROUP, local_heads, HEAD_DIM)
    )
    mixed = attend(query, keys_new, values_new, keys_cache, values_cache, request_row, owner)
    mixed = mixed.reshape(TOK_GROUP, local_heads * HEAD_DIM)
    own_sum = lax.psum_scatter(
        jnp.dot(mixed, output_weight, preferred_element_type=jnp.float32),
        "mp",
        scatter_dimension=0,
        tiled=True,
    )
    state_own = (tokens.astype(jnp.float32) + own_sum).astype(jnp.bfloat16)
    normed_own = layer_norm(state_own.astype(jnp.float32)).astype(jnp.bfloat16)
    normed_two = lax.all_gather(normed_own, "mp", axis=0, tiled=True)

    def add_rows(piece):
        return jnp.dot(normed_two, piece, preferred_element_type=jnp.float32)

    gate = add_rows(lax.all_gather(gate_weight, "dp", axis=0, tiled=True))
    upward = add_rows(lax.all_gather(up_weight, "dp", axis=0, tiled=True))
    activated = (jax.nn.silu(gate) * upward).astype(jnp.bfloat16)
    terms = lax.dot_general(
        activated,
        lax.all_gather(down_weight, "dp", axis=0, tiled=True),
        (((1,), (1,)), ((), ())),
        preferred_element_type=jnp.float32,
    )
    hidden_own = lax.psum_scatter(terms, "mp", scatter_dimension=0, tiled=True)
    return (state_own.astype(jnp.float32) + hidden_own).astype(jnp.bfloat16)


def solution(mesh):
    in_specs = (
        P(("rep", "dp", "mp"), None),
        P(("rep", "dp"), None),
        P(("rep", "dp", "mp"), None),
        P(),
        P("dp"),
        P(None, "mp"),
        P(None, "mp"),
        P(None, "mp"),
        P("mp", None),
        P("dp", "mp"),
        P("dp", "mp"),
        P("dp", "mp"),
    )
    out_specs = P(("rep", "dp", "mp"), None)
    return jax.shard_map(local, mesh=mesh, in_specs=in_specs, out_specs=out_specs, check_vma=False)
```

profile of v0, /device:TPU:1, one launch (start us, length us, event | category | flops | bytes accessed | tf_op | source)
XLA Modules:
  0.0 476.3 jit_solution(9177185737929228484)
XLA Ops:
  6.5 1.8 copy.71
  8.3 7.8 %collective-permute-start = (bf16[128,4096]{0,1:T(8,128)(2,1)S(1)}, bf16[128,4096]{0,1:T(8,128)(2,1)}, u32[]{:S(2)}, u32[]{:S(2)}) collective-permute-start(bf16[128,4096]{0,1:T(8,128)(2,1)S(1)} %copy.71), channel_id=1, source_target_pairs={{0,128},{128,0},{1,129},{129,1},{2,130},{130,2},{3,131},{131,3},{4... | collective-permute-start | bytes 3145736 | tf_op jit(solution)/shard_map/ppermute | solution.py:19
  16.8 0.8 constant_dynamic-slice_fusion
  17.7 0.7 reduce
  18.5 0.2 reduce-window_1_clone.1
  19.2 25.3 %collective-permute-done = bf16[128,4096]{0,1:T(8,128)(2,1)} collective-permute-done((bf16[128,4096]{0,1:T(8,128)(2,1)S(1)}, bf16[128,4096]{0,1:T(8,128)(2,1)}, u32[]{:S(2)}, u32[]{:S(2)}) %collective-permute-start) | collective-permute-done | bytes 1048608 | tf_op jit(solution)/shard_map/ppermute | solution.py:19
  44.6 1.3 broadcast_select_fusion
  45.9 9.5 %copy.73 = bf16[128,2,2048]{0,1,2:T(2,128)(2,1)} copy(bf16[128,2,2048]{0,2,1:T(8,128)(2,1)S(1)} %bitcast.28) | data formatting | bytes 2097152 | tf_op jit(solution)/shard_map/reshape | solution.py:101
  55.4 4.7 all-to-all-start
  60.2 0.8 pad_add_fusion
  61.0 1.5 multiply_cosine_fusion
  62.5 7.3 %all-to-all-done = bf16[128,2,2048]{0,1,2:T(2,128)(2,1)S(1)} async-done(((bf16[128,2,2048]{0,1,2:T(2,128)(2,1)}), bf16[128,2,2048]{0,1,2:T(2,128)(2,1)S(1)}, u32[]{:S(2)}, u32[]{:S(2)}) %all-to-all-start) | async-done | bytes 1048608 | tf_op jit(solution)/shard_map/all_to_all | solution.py:100
  69.8 1.1 copy.74
  70.9 1.5 copy.75
  72.4 1.0 fusion.40
  73.5 1.3 copy.81
  74.7 0.3 copy.84
  75.0 2.0 copy.76
  77.0 1.8 convert_reduce_fusion
  78.9 2.0 fusion.4
  80.8 3.6 fusion.35
  84.4 1.4 reshape.153
  85.8 4.0 fusion.37
  89.8 2.3 reshape.151
  92.1 3.9 convolution_convert_fusion
  95.9 1.9 copy.85
  97.8 2.3 fusion.41
  100.2 0.4 subtract_convert_fusion.1
  100.6 0.9 fusion.16
  101.6 2.7 fusion.43
  104.3 1.1 fusion.10
  105.4 2.7 fusion.44
  108.1 0.3 all-gather.8.cloned.1.call-start
  108.4 61.6 %reduce-scatter.3.cloned.1.call-done = f32[96,2048]{1,0:T(8,128)} async-done(((f32[384,2048]{1,0:T(8,128)}), f32[96,2048]{1,0:T(8,128)}) %reduce-scatter.3.cloned.1.call-update) | async-done | bytes 786448 | tf_op jit(solution)/shard_map/reduce_scatter | solution.py:123
  169.9 1.3 convert_reduce_fusion.1
  171.3 0.3 fusion.22
  171.6 1.0 fusion.23
  172.6 0.5 all-gather.10.cloned.1.call-update
  173.2 0.5 all-gather.12.cloned.1.call-update
  173.8 0.5 all-gather.14.cloned.1.call-update
  174.4 27.1 %all-gather.8.cloned.1.call-done = bf16[384,2048]{1,0:T(8,128)(2,1)} async-done(((bf16[96,2048]{1,0:T(8,128)(2,1)}), bf16[384,2048]{1,0:T(8,128)(2,1)}) %all-gather.8.cloned.1.call-update) | async-done | bytes 1572880 | tf_op jit(solution)/shard_map/all_gather | solution.py:131
  201.5 71.4 %all-gather.10.cloned.1.call-done = bf16[2048,2048]{1,0:T(8,128)(2,1)} async-done(((bf16[64,2048]{1,0:T(8,128)(2,1)}), bf16[2048,2048]{1,0:T(8,128)(2,1)}) %all-gather.10.cloned.1.call-update) | async-done | bytes 8388624 | tf_op jit(solution)/shard_map/all_gather | solution.py:136
  272.9 9.0 %fusion.45 = f32[384,2048]{1,0:T(8,128)} fusion(bf16[384,2048]{1,0:T(8,128)(2,1)} %all-gather.8.cloned.1.call-done, bf16[2048,2048]{1,0:T(8,128)(2,1)} %all-gather.10.cloned.1.call-done), kind=kOutput, calls=%fused_computation.76 | convolution fusion | flops 3221225472 | bytes 13107200 | tf_op jit(solution)/shard_map/dot_general | solution.py:134
  281.9 60.6 %all-gather.12.cloned.1.call-done = bf16[2048,2048]{1,0:T(8,128)(2,1)} async-done(((bf16[64,2048]{1,0:T(8,128)(2,1)}), bf16[2048,2048]{1,0:T(8,128)(2,1)}) %all-gather.12.cloned.1.call-update) | async-done | bytes 8388624 | tf_op jit(solution)/shard_map/all_gather | solution.py:137
  342.5 69.7 %all-gather.14.cloned.1.call-done = bf16[2048,2048]{1,0:T(8,128)(2,1)} async-done(((bf16[64,2048]{1,0:T(8,128)(2,1)}), bf16[2048,2048]{1,0:T(8,128)(2,1)}) %all-gather.14.cloned.1.call-update) | async-done | bytes 8388624 | tf_op jit(solution)/shard_map/all_gather | solution.py:141
  412.2 15.9 %fusion.25 = f32[384,2048]{1,0:T(8,128)} fusion(bf16[2048,2048]{1,0:T(8,128)(2,1)} %all-gather.14.cloned.1.call-done, f32[384,2048]{1,0:T(8,128)} %fusion.45, bf16[384,2048]{1,0:T(8,128)(2,1)} %all-gather.8.cloned.1.call-done, bf16[2048,2048]{1,0:T(8,128)(2,1)} %all-gather.12.cloned.1.call-done), kind=kOutput, calls=%fused_computation.42 | convolution fusion | flops 6447169536 | bytes 24641536 | tf_op jit(solution)/shard_map/dot_general | solution.py:139
  428.1 39.4 %reduce-scatter.5.cloned.1.call-done = f32[96,2048]{1,0:T(8,128)} async-done(((f32[384,2048]{1,0:T(8,128)}), f32[96,2048]{1,0:T(8,128)}) %reduce-scatter.5.cloned.1.call-update) | async-done | bytes 786448 | tf_op jit(solution)/shard_map/reduce_scatter | solution.py:145
  467.5 2.0 fusion.24
  (43 shorter events, 1.2 us)
Async XLA Ops:
  6.5 98.8 %copy-start = (bf16[512,2048]{1,0:T(8,128)(2,1)S(1)}, bf16[512,2048]{1,0:T(8,128)(2,1)}, u32[]{:S(2)}) copy-start(bf16[512,2048]{1,0:T(8,128)(2,1)} %param.20) | copy-start | bytes 6291460
  6.5 70.5 %all-gather.6.cloned.1.call-start = ((), (), s32[]{:S(2)}) async-start(), calls=%async_computation.3 | async-start | bytes 1966080 | tf_op jit(solution)/shard_map/all_gather | solution.py:105
  8.3 36.3 %collective-permute-start = (bf16[128,4096]{0,1:T(8,128)(2,1)S(1)}, bf16[128,4096]{0,1:T(8,128)(2,1)}, u32[]{:S(2)}, u32[]{:S(2)}) collective-permute-start(bf16[128,4096]{0,1:T(8,128)(2,1)S(1)} %copy.71), channel_id=1, source_target_pairs={{0,128},{128,0},{1,129},{129,1},{2,130},{130,2},{3,131},{131,3},{4... | collective-permute-start | bytes 3145736 | tf_op jit(solution)/shard_map/ppermute | solution.py:19
  55.4 14.5 %all-to-all-start = ((bf16[128,2,2048]{0,1,2:T(2,128)(2,1)}), bf16[128,2,2048]{0,1,2:T(2,128)(2,1)S(1)}, u32[]{:S(2)}, u32[]{:S(2)}) async-start(bf16[128,2,2048]{0,1,2:T(2,128)(2,1)} %copy.73), calls=%async_computation | async-start | bytes 2097152 | tf_op jit(solution)/shard_map/all_to_all | solution.py:100
  60.1 109.8 %reduce-scatter.3.cloned.1.call-start = ((), (), s32[]{:S(2)}) async-start(), calls=%async_computation.4 | async-start | bytes 3932160 | tf_op jit(solution)/shard_map/reduce_scatter | solution.py:123
  77.0 3.8 copy-start.2
  97.8 2.3 copy-start.4
  97.8 2.3 copy-start.5
  100.6 1.0 copy-start.8
  101.6 2.7 copy-start.6
  101.6 2.7 copy-start.7
  105.4 64.5 %copy-start.3 = (bf16[96,2048]{1,0:T(8,128)(2,1)S(1)}, bf16[96,2048]{1,0:T(8,128)(2,1)}, u32[]{:S(2)}) copy-start(bf16[96,2048]{1,0:T(8,128)(2,1)} %param.12) | copy-start | bytes 1179652
  108.1 93.4 %all-gather.8.cloned.1.call-start = ((), (), s32[]{:S(2)}) async-start(), calls=%async_computation.5 | async-start | bytes 1966080 | tf_op jit(solution)/shard_map/all_gather | solution.py:131
  172.6 100.3 %all-gather.10.cloned.1.call-start = ((), (), s32[]{:S(2)}) async-start(), calls=%async_computation.6 | async-start | bytes 8650752 | tf_op jit(solution)/shard_map/all_gather | solution.py:136
  173.1 169.4 %all-gather.12.cloned.1.call-start = ((), (), s32[]{:S(2)}) async-start(), calls=%async_computation.7 | async-start | bytes 8650752 | tf_op jit(solution)/shard_map/all_gather | solution.py:137
  173.7 238.5 %all-gather.14.cloned.1.call-start = ((), (), s32[]{:S(2)}) async-start(), calls=%async_computation.8 | async-start | bytes 8650752 | tf_op jit(solution)/shard_map/all_gather | solution.py:141
  174.3 293.2 %reduce-scatter.5.cloned.1.call-start = ((), (), s32[]{:S(2)}) async-start(), calls=%async_computation.9 | async-start | bytes 3932160 | tf_op jit(solution)/shard_map/reduce_scatter | solution.py:145
  412.2 57.2 %copy-start.1 = (bf16[512,2048]{1,0:T(8,128)(2,1)S(1)}, bf16[512,2048]{1,0:T(8,128)(2,1)}, u32[]{:S(2)}) copy-start(bf16[512,2048]{1,0:T(8,128)(2,1)} %param.20) | copy-start | bytes 6291460
Sparse Core Ops, SparseCore 0:
  16.3 27.0 all-gather.5
  108.2 61.6 reduce-scatter.2
  172.7 28.7 all-gather.7
  203.2 69.6 all-gather.9
  274.6 67.9 all-gather.11
  344.2 67.9 all-gather.13
  428.2 39.2 reduce-scatter.4
where the time goes:
time: 477 us; the launch traced here: 476 us
  waiting for transfers between devices  364 us (76%)
  matrix products  41 us (9%)
  local copies, waits for them, and re-layouts  27.2 us (6%)
  other arithmetic  16.8 us (4%)
  between operations  14.3 us (3%)
  starting transfers between devices  13 us (3%)
    all_gather x1, waiting for transfers between devices, local(): gate = add_rows(lax.all_gather(gate_weight, 'dp', axis=0, tiled=True))  71.4 us
    all_gather x1, waiting for transfers between devices, local(): lax.all_gather(down_weight, 'dp', axis=0, tiled=True)  69.7 us
    reduce_scatter x1, waiting for transfers between devices, local(): lax.psum_scatter(jnp.dot(mixed, output_weight, preferred_element_type=jnp...  61.6 us
    all_gather x1, waiting for transfers between devices, local(): upward = add_rows(lax.all_gather(up_weight, 'dp', axis=0, tiled=True))  60.6 us
    reduce_scatter x1, waiting for transfers between devices, local(): hidden_own = lax.psum_scatter(terms, 'mp', scatter_dimension=0, tiled=True)  39.4 us
    all_gather x1, waiting for transfers between devices, local(): normed_two = lax.all_gather(normed_own, 'mp', axis=0, tiled=True)  27.1 us
    ppermute x1, waiting for transfers between devices, swapped(): return lax.ppermute(value, axis, pairs)  25.3 us
    dot_general x1, matrix products, local(): lax.dot_general(activated, lax.all_gather(down_weight, 'dp', axis=0, tile...  15.9 us
  transfers between devices with their start and end apart: 9, of which 8 were waited for; matrix products, arithmetic and copies ran while one was open for 7% of the time, Pallas kernels for 0%

commit v1 on v0

--- a/solution.py
+++ b/solution.py
@@ -3,6 +3,7 @@
 import jax.numpy as jnp
 from jax import lax
 from jax.sharding import PartitionSpec as P
+from jax.lax import all_to_all, axis_size
 
 D = 2048
 HEADS = 16
@@ -134,7 +135,17 @@
         return jnp.dot(normed_two, piece, preferred_element_type=jnp.float32)
 
     gate = add_rows(lax.all_gather(gate_weight, "dp", axis=0, tiled=True))
-    upward = add_rows(lax.all_gather(up_weight, "dp", axis=0, tiled=True))
+    upward = add_rows(
+        jnp.concatenate(
+            all_to_all(
+                jnp.stack([up_weight for _ in range(axis_size("dp"))]),
+                axis_name="dp",
+                split_axis=0,
+                concat_axis=0,
+            ),
+            0,
+        )
+    )
     activated = (jax.nn.silu(gate) * upward).astype(jnp.bfloat16)
     terms = lax.dot_general(
         activated,

time: 477 us -> 524 us (1.099)
  waiting for transfers between devices: 364 us -> 399 us
  starting transfers between devices: 13 us -> 21 us
    all_gather x1, waiting for transfers between devices: 71.4 us -> 175 us  [local(): gate = add_rows(lax.all_gather(gate_weight, 'dp', axis=0, tiled=True))]
    all_gather x1 -> x0, waiting for transfers between devices: 60.6 us -> none  [local(): upward = add_rows(lax.all_gather(up_weight, 'dp', axis=0, tiled=True))]
    all_to_all x0 -> x1, waiting for transfers between devices: none -> 48.5 us  [local(): all_to_all(jnp.stack([up_weight for _ in range(axis_size('dp'))]), axis_n...]
    all_gather x1, waiting for transfers between devices: 69.7 us -> 27.1 us  [local(): lax.all_gather(down_weight, 'dp', axis=0, tiled=True)]
    all_gather x1, waiting for transfers between devices: 27.1 us -> 15.4 us  [local(): normed_two = lax.all_gather(normed_own, 'mp', axis=0, tiled=True)]
    all_to_all x0 -> x1, starting transfers between devices: none -> 8.04 us  [local(): all_to_all(jnp.stack([up_weight for _ in range(axis_size('dp'))]), axis_n...]
where the time goes in v1:
time: 524 us; the launch traced here: 523 us
  waiting for transfers between devices  399 us (76%)
  matrix products  40.8 us (8%)
  local copies, waits for them, and re-layouts  31.5 us (6%)
  starting transfers between devices  21 us (4%)
  other arithmetic  16.8 us (3%)
  between operations  14.3 us (3%)
    all_gather x1, waiting for transfers between devices, local(): gate = add_rows(lax.all_gather(gate_weight, 'dp', axis=0, tiled=True))  175 us
    reduce_scatter x1, waiting for transfers between devices, local(): lax.psum_scatter(jnp.dot(mixed, output_weight, preferred_element_type=jnp...  61.6 us
    all_to_all x1, waiting for transfers between devices, local(): all_to_all(jnp.stack([up_weight for _ in range(axis_size('dp'))]), axis_n...  48.5 us
    reduce_scatter x1, waiting for transfers between devices, local(): hidden_own = lax.psum_scatter(terms, 'mp', scatter_dimension=0, tiled=True)  37.7 us
    all_gather x1, waiting for transfers between devices, local(): lax.all_gather(down_weight, 'dp', axis=0, tiled=True)  27.1 us
    ppermute x1, waiting for transfers between devices, swapped(): return lax.ppermute(value, axis, pairs)  25.3 us
    dot_general x1, matrix products, local(): lax.dot_general(activated, lax.all_gather(down_weight, 'dp', axis=0, tile...  15.9 us
    all_gather x1, waiting for transfers between devices, local(): normed_two = lax.all_gather(normed_own, 'mp', axis=0, tiled=True)  15.4 us
  transfers between devices with their start and end apart: 9, of which 8 were waited for; matrix products, arithmetic and copies ran while one was open for 7% of the time, Pallas kernels for 0%

profile of v1, /device:TPU:1, one launch (start us, length us, event | category | flops | bytes accessed | tf_op | source)
XLA Modules:
  0.0 523.2 jit_solution(1397692109149934248)
XLA Ops:
  6.5 1.8 copy.71
  8.3 7.8 %collective-permute-start = (bf16[128,4096]{0,1:T(8,128)(2,1)S(1)}, bf16[128,4096]{0,1:T(8,128)(2,1)}, u32[]{:S(2)}, u32[]{:S(2)}) collective-permute-start(bf16[128,4096]{0,1:T(8,128)(2,1)S(1)} %copy.71), channel_id=1, source_target_pairs={{0,128},{128,0},{1,129},{129,1},{2,130},{130,2},{3,131},{131,3},{4... | collective-permute-start | bytes 3145736 | tf_op jit(solution)/shard_map/ppermute | solution.py:20
  16.8 0.8 constant_dynamic-slice_fusion
  17.7 0.7 reduce
  19.2 25.3 %collective-permute-done = bf16[128,4096]{0,1:T(8,128)(2,1)} collective-permute-done((bf16[128,4096]{0,1:T(8,128)(2,1)S(1)}, bf16[128,4096]{0,1:T(8,128)(2,1)}, u32[]{:S(2)}, u32[]{:S(2)}) %collective-permute-start) | collective-permute-done | bytes 1048608 | tf_op jit(solution)/shard_map/ppermute | solution.py:20
  44.6 1.3 broadcast_select_fusion
  45.9 9.5 %copy.73 = bf16[128,2,2048]{0,1,2:T(2,128)(2,1)} copy(bf16[128,2,2048]{0,2,1:T(8,128)(2,1)S(1)} %bitcast.29) | data formatting | bytes 2097152 | tf_op jit(solution)/shard_map/reshape | solution.py:102
  55.4 4.7 all-to-all-start
  60.2 0.8 pad_add_fusion
  61.0 1.5 multiply_cosine_fusion
  62.5 7.3 %all-to-all-done = bf16[128,2,2048]{0,1,2:T(2,128)(2,1)S(1)} async-done(((bf16[128,2,2048]{0,1,2:T(2,128)(2,1)}), bf16[128,2,2048]{0,1,2:T(2,128)(2,1)S(1)}, u32[]{:S(2)}, u32[]{:S(2)}) %all-to-all-start) | async-done | bytes 1048608 | tf_op jit(solution)/shard_map/all_to_all | solution.py:101
  69.8 1.1 copy.74
  70.9 1.5 copy.75
  72.4 1.0 fusion.40
  73.5 1.3 copy.81
  74.7 0.3 copy.84
  75.0 2.0 copy.76
  77.0 1.8 convert_reduce_fusion
  78.9 2.0 fusion.4
  80.8 3.6 fusion.35
  84.4 1.4 reshape.158
  85.8 4.0 fusion.37
  89.8 2.3 reshape.156
  92.1 3.9 convolution_convert_fusion
  95.9 1.9 copy.85
  97.8 2.3 fusion.41
  100.2 0.4 subtract_convert_fusion.1
  100.6 0.9 fusion.16
  101.6 2.7 fusion.43
  104.3 1.1 fusion.10
  105.4 2.7 fusion.44
  108.1 0.3 all-gather.7.cloned.1.call-start
  108.4 61.6 %reduce-scatter.3.cloned.1.call-done = f32[96,2048]{1,0:T(8,128)} async-done(((f32[384,2048]{1,0:T(8,128)}), f32[96,2048]{1,0:T(8,128)}) %reduce-scatter.3.cloned.1.call-update) | async-done | bytes 786448 | tf_op jit(solution)/shard_map/reduce_scatter | solution.py:124
  169.9 1.3 convert_reduce_fusion.1
  171.3 0.3 fusion.22
  171.6 1.0 fusion.23
  172.6 0.5 all-gather.9.cloned.1.call-update
  173.2 4.3 stack.2
  177.4 8.0 %all-to-all-start.1 = ((bf16[32,64,2048]{2,1,0:T(8,128)(2,1)}), bf16[32,64,2048]{2,1,0:T(8,128)(2,1)}, u32[]{:S(2)}, u32[]{:S(2)}) async-start(bf16[32,64,2048]{2,1,0:T(8,128)(2,1)} %stack.2), calls=%async_computation.2 | async-start | bytes 16777216 | tf_op jit(solution)/shard_map/all_to_all | solution.py:140
  185.5 0.5 all-gather.11.cloned.1.call-update
  186.1 15.4 %all-gather.7.cloned.1.call-done = bf16[384,2048]{1,0:T(8,128)(2,1)} async-done(((bf16[96,2048]{1,0:T(8,128)(2,1)}), bf16[384,2048]{1,0:T(8,128)(2,1)}) %all-gather.7.cloned.1.call-update) | async-done | bytes 1572880 | tf_op jit(solution)/shard_map/all_gather | solution.py:132
  201.5 174.8 %all-gather.9.cloned.1.call-done = bf16[2048,2048]{1,0:T(8,128)(2,1)} async-done(((bf16[64,2048]{1,0:T(8,128)(2,1)}), bf16[2048,2048]{1,0:T(8,128)(2,1)}) %all-gather.9.cloned.1.call-update) | async-done | bytes 8388624 | tf_op jit(solution)/shard_map/all_gather | solution.py:137
  376.3 8.9 %fusion.45 = f32[384,2048]{1,0:T(8,128)} fusion(bf16[384,2048]{1,0:T(8,128)(2,1)} %all-gather.7.cloned.1.call-done, bf16[2048,2048]{1,0:T(8,128)(2,1)} %all-gather.9.cloned.1.call-done), kind=kOutput, calls=%fused_computation.76 | convolution fusion | flops 3221225472 | bytes 13107200 | tf_op jit(solution)/shard_map/dot_general | solution.py:135
  385.2 48.5 %all-to-all-done.1 = bf16[32,64,2048]{2,1,0:T(8,128)(2,1)} async-done(((bf16[32,64,2048]{2,1,0:T(8,128)(2,1)}), bf16[32,64,2048]{2,1,0:T(8,128)(2,1)}, u32[]{:S(2)}, u32[]{:S(2)}) %all-to-all-start.1) | async-done | bytes 8388640 | tf_op jit(solution)/shard_map/all_to_all | solution.py:140
  433.7 27.1 %all-gather.11.cloned.1.call-done = bf16[2048,2048]{1,0:T(8,128)(2,1)} async-done(((bf16[64,2048]{1,0:T(8,128)(2,1)}), bf16[2048,2048]{1,0:T(8,128)(2,1)}) %all-gather.11.cloned.1.call-update) | async-done | bytes 8388624 | tf_op jit(solution)/shard_map/all_gather | solution.py:152
  460.8 15.9 %fusion.25 = f32[384,2048]{1,0:T(8,128)} fusion(bf16[2048,2048]{1,0:T(8,128)(2,1)} %all-gather.11.cloned.1.call-done, f32[384,2048]{1,0:T(8,128)} %fusion.45, bf16[384,2048]{1,0:T(8,128)(2,1)} %all-gather.7.cloned.1.call-done, bf16[2048,2048]{1,0:T(8,128)(2,1)} %bitcast.14), kind=kOutput, calls=%fused_computation.42 | convolution fusion | flops 6447169536 | bytes 24641536 | tf_op jit(solution)/shard_map/dot_general | solution.py:150
  476.7 37.7 %reduce-scatter.5.cloned.1.call-done = f32[96,2048]{1,0:T(8,128)} async-done(((f32[384,2048]{1,0:T(8,128)}), f32[96,2048]{1,0:T(8,128)}) %reduce-scatter.5.cloned.1.call-update) | async-done | bytes 786448 | tf_op jit(solution)/shard_map/reduce_scatter | solution.py:156
  514.4 2.0 fusion.24
  (45 shorter events, 1.4 us)
Async XLA Ops:
  6.5 98.8 %copy-start = (bf16[512,2048]{1,0:T(8,128)(2,1)S(1)}, bf16[512,2048]{1,0:T(8,128)(2,1)}, u32[]{:S(2)}) copy-start(bf16[512,2048]{1,0:T(8,128)(2,1)} %param.20) | copy-start | bytes 6291460
  6.5 70.5 %all-gather.5.cloned.1.call-start = ((), (), s32[]{:S(2)}) async-start(), calls=%async_computation.4 | async-start | bytes 1966080 | tf_op jit(solution)/shard_map/all_gather | solution.py:106
  8.3 36.3 %collective-permute-start = (bf16[128,4096]{0,1:T(8,128)(2,1)S(1)}, bf16[128,4096]{0,1:T(8,128)(2,1)}, u32[]{:S(2)}, u32[]{:S(2)}) collective-permute-start(bf16[128,4096]{0,1:T(8,128)(2,1)S(1)} %copy.71), channel_id=1, source_target_pairs={{0,128},{128,0},{1,129},{129,1},{2,130},{130,2},{3,131},{131,3},{4... | collective-permute-start | bytes 3145736 | tf_op jit(solution)/shard_map/ppermute | solution.py:20
  55.4 14.5 %all-to-all-start = ((bf16[128,2,2048]{0,1,2:T(2,128)(2,1)}), bf16[128,2,2048]{0,1,2:T(2,128)(2,1)S(1)}, u32[]{:S(2)}, u32[]{:S(2)}) async-start(bf16[128,2,2048]{0,1,2:T(2,128)(2,1)} %copy.73), calls=%async_computation | async-start | bytes 2097152 | tf_op jit(solution)/shard_map/all_to_all | solution.py:101
  60.1 109.8 %reduce-scatter.3.cloned.1.call-start = ((), (), s32[]{:S(2)}) async-start(), calls=%async_computation.5 | async-start | bytes 3932160 | tf_op jit(solution)/shard_map/reduce_scatter | solution.py:124
  77.0 3.8 copy-start.2
  97.8 2.3 copy-start.4
  97.8 2.3 copy-start.5
  100.6 1.0 copy-start.8
  101.6 2.7 copy-start.6
  101.6 2.7 copy-start.7
  105.4 64.6 %copy-start.3 = (bf16[96,2048]{1,0:T(8,128)(2,1)S(1)}, bf16[96,2048]{1,0:T(8,128)(2,1)}, u32[]{:S(2)}) copy-start(bf16[96,2048]{1,0:T(8,128)(2,1)} %param.12) | copy-start | bytes 1179652
  108.1 65.1 %copy-start.9 = (bf16[64,2048]{1,0:T(8,128)(2,1)S(1)}, bf16[64,2048]{1,0:T(8,128)(2,1)}, u32[]{:S(2)}) copy-start(bf16[64,2048]{1,0:T(8,128)(2,1)} %param.22) | copy-start | bytes 786436
  108.1 93.4 %all-gather.7.cloned.1.call-start = ((), (), s32[]{:S(2)}) async-start(), calls=%async_computation.6 | async-start | bytes 1966080 | tf_op jit(solution)/shard_map/all_gather | solution.py:132
  172.6 203.7 %all-gather.9.cloned.1.call-start = ((), (), s32[]{:S(2)}) async-start(), calls=%async_computation.7 | async-start | bytes 8650752 | tf_op jit(solution)/shard_map/all_gather | solution.py:137
  177.4 256.3 %all-to-all-start.1 = ((bf16[32,64,2048]{2,1,0:T(8,128)(2,1)}), bf16[32,64,2048]{2,1,0:T(8,128)(2,1)}, u32[]{:S(2)}, u32[]{:S(2)}) async-start(bf16[32,64,2048]{2,1,0:T(8,128)(2,1)} %stack.2), calls=%async_computation.2 | async-start | bytes 16777216 | tf_op jit(solution)/shard_map/all_to_all | solution.py:140
  185.5 275.3 %all-gather.11.cloned.1.call-start = ((), (), s32[]{:S(2)}) async-start(), calls=%async_computation.8 | async-start | bytes 8650752 | tf_op jit(solution)/shard_map/all_gather | solution.py:152
  186.1 328.3 %reduce-scatter.5.cloned.1.call-start = ((), (), s32[]{:S(2)}) async-start(), calls=%async_computation.9 | async-start | bytes 3932160 | tf_op jit(solution)/shard_map/reduce_scatter | solution.py:156
  460.8 55.6 %copy-start.1 = (bf16[512,2048]{1,0:T(8,128)(2,1)S(1)}, bf16[512,2048]{1,0:T(8,128)(2,1)}, u32[]{:S(2)}) copy-start(bf16[512,2048]{1,0:T(8,128)(2,1)} %param.20) | copy-start | bytes 6291460
Sparse Core Ops, SparseCore 0:
  16.3 27.0 all-gather.4
  108.2 61.6 reduce-scatter.2
  172.7 28.7 all-gather.6
  203.2 173.0 all-gather.8
  378.0 82.7 all-gather.10
  476.8 37.5 reduce-scatter.4
